TPU v7x, 32 devices: a whole 2x2x4 slice. The times are simulated.
32 devices in a mesh: dp: 4 (over y, x), seq: 8 (over z, core).
Axes of the slice: x: 2, y: 2, z: 4, core: 2. Of those that a mesh axis runs over, the one named last changes fastest.
Arguments:
- queries: bfloat16 [4096, 4096], P('seq', 'dp'), may hold values from -6 to 6
- keys: bfloat16 [4096, 4096], P('seq', 'dp'), may hold values from -6 to 6
- values: bfloat16 [4096, 4096], P('seq', 'dp'), may hold values from -6 to 6
- out_grad: bfloat16 [4096, 4096], P('seq', 'dp'), may hold values from -6 to 6
- gain: float32 [4096], P('dp'), may hold values from 0.5 to 1.5
- decay_index: int32 [32], P('dp'), may hold values from 0 to 15
- bounds: int32 [3], replicated, may hold values from 896 to 3200, as said below
Outputs:
- query_grad: bfloat16 [4096, 4096], P('seq', 'dp')
- key_grad: bfloat16 [4096, 4096], P('seq', 'dp')
- value_grad: bfloat16 [4096, 4096], P('seq', 'dp')
- gain_grad: float32 [4096], P(('dp', 'seq'))
Inputs may be any that keep to these rules, and one draw needn't show every extreme that they name: `bounds`: the 3 positions rise strictly and lie inside the stream; token p starts a new episode when p is one of them.
All inputs are finite; a program needn't handle non-finite values.
Results may differ from a plain program's by a relative error of at most 0.0063.
Values sent between devices are 32-bit elements; how exact they have to be, the bound alone decides.
A program may use at most 128 MiB of HBM per device.

v0:
```python
import jax
import jax.numpy as jnp
from jax import lax
from jax.sharding import PartitionSpec as P


def carried_in(array, axis, combine, identity, reverse):
    size, position = (lax.axis_size(axis), lax.axis_index(axis))
    everything = jax.tree.map(lambda part: lax.all_gather(part, axis), array)
    start = jax.tree.map(
        lambda part, zero: jnp.broadcast_to(jnp.asarray(zero, part.dtype), part.shape),
        array,
        identity,
    )

    def hop(k, before):
        at = size - 1 - k if reverse else k
        reached = at > position if reverse else at < position
        new = combine(before, jax.tree.map(lambda part: part[at], everything))
        return jax.tree.map(lambda a, b: jnp.where(reached, a, b), new, before)

    return lax.fori_loop(0, size, hop, start)


def decay_rates(decay_index, stream_length):
    level = decay_index.astype(jnp.float32)
    slow_rate = -0.25 * jnp.exp(level / 7.0 * jnp.log(8.0)) / stream_length
    lowest = jnp.log(4.0 / stream_length)
    fast_rate = -jnp.exp(lowest + (level - 8.0) / 7.0 * (jnp.log(1.0 / 32.0) - lowest))
    return jnp.where(decay_index < 8, slow_rate, fast_rate)


def shard_masks(rates, bound_row, first_row, tok_rows):
    places = first_row + jnp.arange(tok_rows, dtype=jnp.int32)
    episode = jnp.sum((bound_row[None, :] <= places[:, None]).astype(jnp.int32), axis=1)
    before = jnp.sum((bound_row <= first_row - 1).astype(jnp.int32))
    enter_mask = (episode == before).astype(jnp.float32)
    leave_mask = (episode == episode[tok_rows - 1]).astype(jnp.float32)
    whole_mask = (episode[tok_rows - 1] == before).astype(jnp.float32)
    local_pos = jnp.arange(tok_rows, dtype=jnp.float32)
    enter_decay = jnp.exp(rates[None, :] * (local_pos[:, None] + 1.0)) * enter_mask[:, None]
    leave_decay = (
        jnp.exp(rates[None, :] * (tok_rows - 1.0 - local_pos[:, None])) * leave_mask[:, None]
    )
    passing_decay = jnp.exp(rates * tok_rows) * whole_mask
    spacing = local_pos[:, None] - local_pos[None, :]
    allowed = (spacing >= 0.0) & (episode[:, None] == episode[None, :])
    weights = jnp.where(
        allowed[None], jnp.exp(rates[:, None, None] * jnp.maximum(spacing, 0.0)[None]), 0.0
    )
    return (enter_decay, leave_decay, passing_decay, weights)


def combine_states(earlier, later):
    return (earlier[0] * later[0], later[0][:, None, None] * earlier[1] + later[1])


def shards(queries, keys, values, out_grad, gain, decay_index, bounds):
    tok_rows = queries.shape[0]
    feature_width = queries.shape[1]
    head_count = decay_index.shape[0]
    head_size = feature_width // head_count
    all_features = float(feature_width * lax.axis_size("dp"))
    seq_devices = lax.axis_size("seq")
    first_row = lax.axis_index("seq") * tok_rows
    rates = decay_rates(decay_index, float(tok_rows * seq_devices))
    query_rows = queries.reshape(tok_rows, head_count, head_size)
    key_rows = keys.reshape(tok_rows, head_count, head_size)
    value_rows = values.reshape(tok_rows, head_count, head_size)
    grad_wide_in = out_grad.astype(jnp.float32)
    enter_decay, leave_decay, passing_decay, weights = shard_masks(
        rates, bounds, first_row, tok_rows
    )
    decayed_keys = (leave_decay[:, :, None] * key_rows.astype(jnp.float32)).astype(jnp.bfloat16)
    state_local = jnp.einsum(
        "the,thf->hef", decayed_keys, value_rows, preferred_element_type=jnp.float32
    )
    ones_init = jnp.ones((head_count,), jnp.float32)
    zero_state = jnp.zeros((head_count, head_size, head_size), jnp.float32)
    state_in = carried_in(
        (passing_decay, state_local), "seq", combine_states, (ones_init, zero_state), False
    )[1]
    state_low = state_in.astype(jnp.bfloat16)
    scores = jnp.einsum("the,she->hts", query_rows, key_rows, preferred_element_type=jnp.float32)
    mixing = (scores * weights).astype(jnp.bfloat16)
    attended = jnp.einsum("hts,shf->thf", mixing, value_rows, preferred_element_type=jnp.float32)
    attended = attended + enter_decay[:, :, None] * jnp.einsum(
        "the,hef->thf", query_rows, state_low, preferred_element_type=jnp.float32
    )
    flat = attended.reshape(tok_rows, feature_width)
    gained = grad_wide_in * gain[None, :]
    square_total = lax.psum(jnp.sum(flat * flat, axis=1), "dp")
    inverse_rms = lax.rsqrt(square_total / all_features + 1e-06)[:, None]
    normed = flat * inverse_rms
    cross_total = lax.psum(jnp.sum(gained * normed, axis=1), "dp")
    cross_mean = (cross_total / all_features)[:, None]
    grad_flat = inverse_rms * (gained - normed * cross_mean)
    grad_mixed = grad_flat.astype(jnp.bfloat16).reshape(tok_rows, head_count, head_size)
    decayed_queries = (enter_decay[:, :, None] * query_rows.astype(jnp.float32)).astype(
        jnp.bfloat16
    )
    state_grad_local = jnp.einsum(
        "the,thf->hef", decayed_queries, grad_mixed, preferred_element_type=jnp.float32
    )
    state_grad_end = carried_in(
        (passing_decay, state_grad_local), "seq", combine_states, (ones_init, zero_state), True
    )[1]
    state_grad_low = state_grad_end.astype(jnp.bfloat16)
    gain_term = jnp.sum(grad_wide_in * normed, axis=0)
    gain_part = lax.psum_scatter(gain_term, "seq", scatter_dimension=0, tiled=True)
    grad_scores = jnp.einsum(
        "thf,shf->hts", grad_mixed, value_rows, preferred_element_type=jnp.float32
    )
    grad_mixing = (grad_scores * weights).astype(jnp.bfloat16)
    query_grad = jnp.einsum(
        "hts,she->the", grad_mixing, key_rows, preferred_element_type=jnp.float32
    )
    query_grad = query_grad + enter_decay[:, :, None] * jnp.einsum(
        "thf,hef->the", grad_mixed, state_low, preferred_element_type=jnp.float32
    )
    key_grad = jnp.einsum(
        "hts,the->she", grad_mixing, query_rows, preferred_element_type=jnp.float32
    )
    key_grad = key_grad + leave_decay[:, :, None] * jnp.einsum(
        "thf,hef->the", value_rows, state_grad_low, preferred_element_type=jnp.float32
    )
    value_grad = jnp.einsum("hts,thf->shf", mixing, grad_mixed, preferred_element_type=jnp.float32)
    value_grad = value_grad + leave_decay[:, :, None] * jnp.einsum(
        "the,hef->thf", key_rows, state_grad_low, preferred_element_type=jnp.float32
    )
    out_shape = (tok_rows, feature_width)
    return (
        query_grad.reshape(out_shape).astype(jnp.bfloat16),
        key_grad.reshape(out_shape).astype(jnp.bfloat16),
        value_grad.reshape(out_shape).astype(jnp.bfloat16),
        gain_part,
    )


def solution(mesh):
    return jax.shard_map(
        shards,
        mesh=mesh,
        in_specs=(
            P("seq", "dp"),
            P("seq", "dp"),
            P("seq", "dp"),
            P("seq", "dp"),
            P("dp"),
            P("dp"),
            P(),
        ),
        out_specs=(P("seq", "dp"), P("seq", "dp"), P("seq", "dp"), P(("dp", "seq"))),
        check_vma=False,
    )
```

profile of v0, /device:TPU:0, one launch (start us, length us, event | category | flops | bytes accessed | tf_op | source)
XLA Modules:
  0.0 181.4 jit_solution(4440879559795362378)
XLA Ops:
  7.2 0.0 copy-start
  7.2 0.0 all-gather.6.cloned.1.call-start
  7.3 0.8 convert_reduce_fusion
  8.1 0.6 slice.4
  8.7 1.3 fusion.36
  10.0 1.3 compare_convert_fusion
  12.6 1.5 copy.52
  14.1 0.7 fusion.37
  15.5 0.1 multiply_dynamic-update-slice_fusion
  15.6 0.1 exponential_multiply_fusion
  15.7 1.3 fusion.15
  17.0 0.0 all-gather.6.cloned.1.call-update
  17.0 0.0 all-gather.8.cloned.1.call-start
  17.1 18.7 %all-reduce = f32[64]{0:T(128)S(1)} all-reduce(f32[64]{0:T(128)S(1)} %get-tuple-element.302), channel_id=2, replica_groups=mesh['dp'=4,'seq'=8] {'seq'}, use_global_device_ids=true, to_apply=%add | all-reduce | flops 64 | bytes 512
  35.8 0.1 reshape.196
  35.9 1.5 copy.51
  37.4 0.2 fusion.25
  37.6 0.3 fusion.27
  37.9 4.0 %multiply_convert_fusion.1 = bf16[8,512,512]{2,1,0:T(8,128)(2,1)S(1)} fusion(f32[512,512]{1,0:T(8,128)S(1)} %fusion.25, f32[8]{0:T(128)S(1)} %get-tuple-element.303, pred[512,512]{1,0:T(8,128)(4,1)S(1)} %fusion.27, bf16[512,8,128]{0,2,1:T(8,128)(2,1)S(1)} %bitcast.102, bf16[512,8,128]{0,2,1:T(8,128)(2,1)} %bitcast.107), kind=kOutput, calls=%fused_computation.7 | convolution fusion | flops 545259520 | bytes 7602208 | tf_op jit(solution)/shard_map/the,she->hts/dot_general | solution.py:84
  42.0 1.9 %copy-done.1 = bf16[8,512,512]{2,1,0:T(8,128)(2,1)} copy-done((bf16[8,512,512]{2,1,0:T(8,128)(2,1)}, bf16[8,512,512]{2,1,0:T(8,128)(2,1)S(1)}, u32[]{:S(2)}) %copy-start.1) | copy-done | bytes 4194328
  43.9 2.9 %fusion.17 = f32[8,512,128]{1,2,0:T(8,128)} fusion(bf16[8,512,512]{2,1,0:T(8,128)(2,1)S(1)} %multiply_convert_fusion.1, bf16[512,1024]{1,0:T(8,128)(2,1)S(1)} %copy-done), kind=kOutput, calls=%fused_computation.33 | convolution fusion | flops 536870912 | bytes 7340032 | tf_op jit(solution)/shard_map/hts,shf->thf/dot_general | solution.py:86
  46.8 20.0 %all-gather.6.cloned.1.call-done = f32[64,128,128]{2,1,0:T(8,128)} async-done(((f32[8,128,128]{2,1,0:T(8,128)}), f32[64,128,128]{2,1,0:T(8,128)}) %all-gather.6.cloned.1.call-update) | async-done | bytes 4194320 | tf_op jit(solution)/shard_map/all_gather | solution.py:9
  66.8 9.7 %while.30 = (s32[]{:T(128)}, f32[8,128,128]{2,1,0:T(8,128)S(1)}, s32[]{:T(128)}, f32[8,8]{1,0:T(8,128)S(1)}, f32[8,8,128,128]{3,2,1,0:T(8,128)}, /*index=5*/s32[]{:T(128)}, s32[]{:T(128)}) while((s32[]{:T(128)}, f32[8,128,128]{2,1,0:T(8,128)S(1)}, s32[]{:T(128)}, f32[8,8]{1,0:T(8,128)S(1)}, f32[8,8,128,128]{3,2,1,0:T(8,128)}, ...), condition=%wide.region_3.4_spmd.clone, body=%wide.region_2.3_spmd.clone.sunk | while | flops 524292 | bytes 1573065 | solution.py:22
  66.8 1.2 fusion.60
  68.0 1.2 fusion.60
  69.2 1.2 fusion.60
  70.4 1.2 fusion.60
  71.6 1.2 fusion.60
  72.9 1.2 fusion.60
  74.1 1.2 fusion.60
  75.3 1.2 fusion.60
  76.5 3.5 %multiply_reduce_fusion = (f32[512]{0:T(512)S(1)}, f32[512,8,128]{0,2,1:T(8,128)}) fusion(bf16[512,8,128]{0,2,1:T(8,128)(2,1)S(1)} %bitcast.103, f32[8,128,128]{2,1,0:T(8,128)S(1)} %get-tuple-element.230, f32[512,8]{0,1:T(8,128)S(1)} %get-tuple-element.309, f32[8,512,128]{1,2,0:T(8,128)} %fusion.17), kind=kOutput, calls=%fused_computation.29 | convolution fusion | flops 136445440 | bytes 5785600 | tf_op jit(solution)/shard_map/the,hef->thf/dot_general | solution.py:87
  80.0 3.0 %copy.59 = f32[512,1024]{1,0:T(8,128)} copy(f32[512,1024]{0,1:T(8,128)} %bitcast.110) | data formatting | bytes 4194304 | tf_op jit(solution)/shard_map/reshape | solution.py:90
  83.0 9.8 %psum.14 = f32[512]{0:T(512)S(1)} all-reduce(f32[512]{0:T(512)S(1)} %get-tuple-element.310), channel_id=1, replica_groups=mesh['dp'=4,'seq'=8] {'dp'}, use_global_device_ids=true, to_apply=%region_5.6 | all-reduce | flops 512 | bytes 4096 | tf_op jit(solution)/shard_map/psum | solution.py:92
  92.8 2.3 %fusion.7 = (f32[1024]{0:T(1024)S(1)}, f32[512]{0:T(512)S(1)}) fusion(bf16[512,1024]{1,0:T(8,128)(2,1)S(1)} %copy-done.9, f32[512,1024]{1,0:T(8,128)} %copy.59, f32[512]{0:T(512)S(1)} %add_rsqrt_fusion, f32[1024]{0:T(1024)S(1)} %copy-done.11), kind=kLoop, calls=%fused_computation.16 | loop fusion | flops 3668480 | bytes 3158016 | tf_op jit(solution)/shard_map/reduce_sum | solution.py:109
  95.1 8.0 %psum.15 = f32[512]{0:T(512)S(1)} all-reduce(f32[512]{0:T(512)S(1)} %get-tuple-element.281), channel_id=1, replica_groups=mesh['dp'=4,'seq'=8] {'dp'}, use_global_device_ids=true, to_apply=%region_7.8 | all-reduce | flops 512 | bytes 4096 | tf_op jit(solution)/shard_map/psum | solution.py:95
  103.1 3.0 %fusion.6 = bf16[512,1024]{1,0:T(8,128)(2,1)} fusion(bf16[512,1024]{1,0:T(8,128)(2,1)S(1)} %copy-done.9, f32[512,1024]{1,0:T(8,128)} %copy.59, f32[512]{0:T(512)S(1)} %broadcast_multiply_fusion, f32[1024]{0:T(1024)S(1)} %copy-done.11, f32[512]{0:T(512)S(1)} %add_rsqrt_fusion), kind=kLoop, calls=%fused_computation.15 | loop fusion | flops 3670016 | bytes 4202496 | tf_op jit(solution)/shard_map/convert_element_type | solution.py:98
  106.1 1.5 copy.77
  107.6 2.4 %fusion.16 = f32[8,128,128]{2,1,0:T(8,128)} fusion(bf16[512,8,128]{0,2,1:T(8,128)(2,1)S(1)} %bitcast.98, bf16[512,8,128]{0,2,1:T(8,128)(2,1)} %bitcast.104, f32[512,8]{0,1:T(8,128)S(1)} %get-tuple-element.309), kind=kOutput, calls=%fused_computation.32 | convolution fusion | flops 135790592 | bytes 2637824 | tf_op jit(solution)/shard_map/the,thf->hef/dot_general | solution.py:102
  110.1 0.0 all-gather.8.cloned.1.call-update
  110.8 3.9 %multiply_convert_fusion = bf16[8,512,512]{2,1,0:T(8,128)(2,1)S(1)} fusion(f32[512,512]{1,0:T(8,128)} %copy-done.10, f32[8]{0:T(128)S(1)} %get-tuple-element.303, pred[512,512]{1,0:T(8,128)(4,1)S(1)} %fusion.27, bf16[512,8,128]{0,2,1:T(8,128)(2,1)S(1)} %bitcast.99, bf16[512,1024]{1,0:T(8,128)(2,1)S(1)} %copy-done), kind=kOutput, calls=%fused_computation.6 | convolution fusion | flops 545259520 | bytes 7602208 | tf_op jit(solution)/shard_map/thf,shf->hts/dot_general | solution.py:111
  114.7 1.5 fusion.38
  116.1 0.5 copy-done.2
  116.6 1.4 fusion.13
  118.0 2.3 %copy.68 = bf16[512,1024]{1,0:T(8,128)(2,1)} copy(bf16[512,1024]{0,1:T(8,128)(2,1)} %bitcast.111) | data formatting | bytes 2097152
  120.3 14.7 %all-reduce.1 = f32[1024]{0:T(1024)S(1)} all-reduce(f32[1024]{0:T(1024)S(1)} %get-tuple-element.280), channel_id=5, replica_groups=mesh['dp'=4,'seq'=8] {'seq'}, use_global_device_ids=true, to_apply=%region_11.12.clone | all-reduce | flops 1024 | bytes 8192
  135.1 0.6 dynamic-slice.2
  135.7 4.3 %fusion.39 = f32[8,128,512]{2,1,0:T(8,128)} fusion(bf16[512,8,128]{0,2,1:T(8,128)(2,1)S(1)} %bitcast.101, bf16[8,512,512]{2,1,0:T(8,128)(2,1)} %copy-done.1), kind=kOutput, calls=%fused_computation.69 | convolution fusion | flops 536870912 | bytes 7340032 | tf_op jit(solution)/shard_map/hts,thf->shf/dot_general | solution.py:127
  139.9 15.4 %all-gather.8.cloned.1.call-done = f32[64,128,128]{2,1,0:T(8,128)} async-done(((f32[8,128,128]{2,1,0:T(8,128)}), f32[64,128,128]{2,1,0:T(8,128)}) %all-gather.8.cloned.1.call-update) | async-done | bytes 4194320 | tf_op jit(solution)/shard_map/all_gather | solution.py:9
  155.4 9.8 %while.31 = (s32[]{:T(128)}, f32[8,128,128]{2,1,0:T(8,128)S(1)}, s32[]{:T(128)}, f32[8,8]{1,0:T(8,128)S(1)}, f32[8,8,128,128]{3,2,1,0:T(8,128)}, /*index=5*/s32[]{:T(128)}, s32[]{:T(128)}, s32[]{:T(128)}, s32[]{:T(128)}) while((s32[]{:T(128)}, f32[8,128,128]{2,1,0:T(8,128)S(1)}, s32[]{:T(128)}, f32[8,8]{1,0:T(8,128)S(1)}, ...), condition=%wide.region_9.10_spmd.clone, body=%wide.region_8.9_spmd.clone.sunk | while | flops 524296 | bytes 1573127 | solution.py:22
  155.4 1.2 fusion.61
  156.6 1.2 fusion.61
  157.8 1.2 fusion.61
  159.0 1.2 fusion.61
  160.3 1.2 fusion.61
  161.5 1.2 fusion.61
  162.7 1.2 fusion.61
  163.9 1.2 fusion.61
  165.1 1.8 fusion.19
  166.9 0.9 copy-done.8
  167.8 0.5 fusion.9
  168.3 1.3 copy.70
  169.6 3.6 %fusion.11 = bf16[512,8,128]{0,2,1:T(8,128)(2,1)S(1)} fusion(f32[8,128,512]{2,1,0:T(8,128)} %fusion.19, bf16[512,8,128]{0,2,1:T(8,128)(2,1)S(1)} %bitcast.105, bf16[8,512,512]{2,1,0:T(8,128)(2,1)} %copy-done.2, f32[512,8]{0,1:T(8,128)S(1)} %get-tuple-element.308), kind=kOutput, calls=%fused_computation.22 | convolution fusion | flops 538443776 | bytes 8404992 | tf_op jit(solution)/shard_map/hts,the->she/dot_general | solution.py:121
  173.2 1.3 copy.69
  (47 shorter events, 0.2 us)
Async XLA Ops:
  7.2 8.5 %copy-start = (bf16[512,1024]{1,0:T(8,128)(2,1)S(1)}, bf16[512,1024]{1,0:T(8,128)(2,1)}, u32[]{:S(2)}) copy-start(bf16[512,1024]{1,0:T(8,128)(2,1)} %param.13) | copy-start | bytes 3145732
  7.2 6.9 %copy-start.12 = (u32[32]{0:T(128)S(1)}, u32[32]{0:T(128)}, u32[]{:S(2)}) copy-start(u32[32]{0:T(128)} %constant.114) | copy-start | bytes 388
  7.2 8.3 %copy-start.13 = (s32[8]{0:T(128)S(1)}, s32[8]{0:T(128)}, u32[]{:S(2)}) copy-start(s32[8]{0:T(128)} %param.16) | copy-start | bytes 100
  7.2 59.6 %all-gather.6.cloned.1.call-start = ((), (), s32[]{:S(2)}) async-start(), calls=%async_computation | async-start | bytes 4718592 | tf_op jit(solution)/shard_map/all_gather | solution.py:9
  14.1 2.9 %copy-start.5 = (bf16[512,1024]{0,1:T(8,128)(2,1)}, bf16[512,1024]{0,1:T(8,128)(2,1)S(1)}, u32[]{:S(2)}) copy-start(bf16[512,1024]{0,1:T(8,128)(2,1)S(1)} %copy.52) | copy-start | bytes 3145732
  17.0 138.3 %all-gather.8.cloned.1.call-start = ((), (), s32[]{:S(2)}) async-start(), calls=%async_computation.1 | async-start | bytes 4718592 | tf_op jit(solution)/shard_map/all_gather | solution.py:9
  37.4 39.1 %copy-start.3 = (bf16[512,1024]{0,1:T(8,128)(2,1)}, bf16[512,1024]{0,1:T(8,128)(2,1)S(1)}, u32[]{:S(2)}) copy-start(bf16[512,1024]{0,1:T(8,128)(2,1)S(1)} %copy.51) | copy-start | bytes 3145732
  37.6 4.4 %copy-start.10 = (f32[512,512]{1,0:T(8,128)}, f32[512,512]{1,0:T(8,128)S(1)}, u32[]{:S(2)}) copy-start(f32[512,512]{1,0:T(8,128)S(1)} %fusion.25) | copy-start | bytes 3145732
  42.0 1.9 %copy-start.1 = (bf16[8,512,512]{2,1,0:T(8,128)(2,1)}, bf16[8,512,512]{2,1,0:T(8,128)(2,1)S(1)}, u32[]{:S(2)}) copy-start(bf16[8,512,512]{2,1,0:T(8,128)(2,1)S(1)} %multiply_convert_fusion.1) | copy-start | bytes 12582916
  80.0 12.8 %copy-start.9 = (bf16[512,1024]{1,0:T(8,128)(2,1)S(1)}, bf16[512,1024]{1,0:T(8,128)(2,1)}, u32[]{:S(2)}) copy-start(bf16[512,1024]{1,0:T(8,128)(2,1)} %param.14) | copy-start | bytes 3145732
  80.0 12.8 %copy-start.11 = (f32[1024]{0:T(1024)S(1)}, f32[1024]{0:T(1024)}, u32[]{:S(2)}) copy-start(f32[1024]{0:T(1024)} %param.15) | copy-start | bytes 12292
  110.8 3.9 %copy-start.6 = (bf16[512,1024]{0,1:T(8,128)(2,1)S(1)}, bf16[512,1024]{0,1:T(8,128)(2,1)}, u32[]{:S(2)}) copy-start(bf16[512,1024]{0,1:T(8,128)(2,1)} %copy-done.5) | copy-start | bytes 3145732
  114.6 2.0 %copy-start.2 = (bf16[8,512,512]{2,1,0:T(8,128)(2,1)}, bf16[8,512,512]{2,1,0:T(8,128)(2,1)S(1)}, u32[]{:S(2)}) copy-start(bf16[8,512,512]{2,1,0:T(8,128)(2,1)S(1)} %multiply_convert_fusion) | copy-start | bytes 12582916
  165.1 1.8 %copy-start.7 = (bf16[512,1024]{0,1:T(8,128)(2,1)S(1)}, bf16[512,1024]{0,1:T(8,128)(2,1)}, u32[]{:S(2)}) copy-start(bf16[512,1024]{0,1:T(8,128)(2,1)} %copy-done.5) | copy-start | bytes 3145732
  165.1 2.7 %copy-start.8 = (f32[8,128,512]{2,1,0:T(8,128)S(1)}, f32[8,128,512]{2,1,0:T(8,128)}, u32[]{:S(2)}) copy-start(f32[8,128,512]{2,1,0:T(8,128)} %fusion.39) | copy-start | bytes 6291460
  168.3 1.3 copy-start.4
Sparse Core Ops, SparseCore 0:
  17.1 49.6 all-gather.5
  110.2 45.0 all-gather.7
where the time goes:
time: 183 us; the launch traced here: 181 us
  blocking collectives  51.3 us (28%)
  waiting for transfers between devices  35.4 us (19%)
  matrix products  31 us (17%)
  other arithmetic  28.2 us (15%)
  local copies, waits for them, and re-layouts  17.8 us (10%)
  between operations  17 us (9%)
    all_gather x2, waiting for transfers between devices, carried_in(): everything = jax.tree.map(lambda part: lax.all_gather(part, axis), array)  35.4 us
    unnamed x2, blocking collectives  33.5 us
    select_n x16, other arithmetic, hop(): return jax.tree.map(lambda a, b: jnp.where(reached, a, b), new, before)  18.8 us
    unnamed x36, local copies, waits for them, and re-layouts  12.5 us
    psum x1, blocking collectives, shards(): square_total = lax.psum(jnp.sum(flat * flat, axis=1), 'dp')  9.81 us
    psum x1, blocking collectives, shards(): cross_total = lax.psum(jnp.sum(gained * normed, axis=1), 'dp')  7.98 us
    dot_general x1, matrix products, shards(): jnp.einsum('hts,thf->shf', mixing, grad_mixed, preferred_element_type=jnp...  4.28 us
    dot_general x1, matrix products, shards(): jnp.einsum('the,she->hts', query_rows, key_rows, preferred_element_type=j...  4.01 us
  transfers between devices with their start and end apart: 2, of which 2 were waited for; matrix products, arithmetic and copies ran while one was open for 13% of the time, Pallas kernels for 0%

commit v1 on v0

v1 whole, which is shorter than its diff:
```python
import functools
import math

import jax
import jax.numpy as jnp
from jax import lax
from jax.experimental import pallas as pl
from jax.experimental.pallas import tpu as pltpu
from jax.sharding import PartitionSpec as P

MESH = pl.DeviceIdType.MESH
F32, BF16 = jnp.float32, jnp.bfloat16
FAR = 1e30
CHUNKS = 2
HEADS_PER_HOP = 2

NN = (((1,), (0,)), ((), ()))
NT = (((1,), (1,)), ((), ()))
TN = (((0,), (0,)), ((), ()))


def dot(a, b, dims):
    return lax.dot_general(a, b, dims, preferred_element_type=F32)


def kernel(
    cfg,
    q_ref, k_ref, v_ref, g_ref, gain_ref, dec_ref, bounds_ref,
    dq_ref, dk_ref, dv_ref, gg_ref,
    rate_ref, pass_ref, enter_ref, leave_ref, dist_ref,
    mix_ref, o_ref, do_ref, dki_ref, dvi_ref, low_ref, dlow_ref,
    sq_ref, cr_ref, stat_ref, gsrc_ref, grecv_ref,
    f_ls, f_lo, f_lr, f_x, f_xs, f_ss, f_sr,
    b_ls, b_lo, b_lr, b_x, b_xs, b_ss, b_sr,
    f_l_sem, f_x_sem, f_s_sem, b_l_sem, b_x_sem, b_s_sem, stat_sem, gain_sem,
):
    tok, heads, size, n_seq, n_dp, scatter = cfg
    half, mid = heads // 2, tok // 2
    rows = size // CHUNKS
    pos, dpi = lax.axis_index("seq"), lax.axis_index("dp")
    core, chip = lax.rem(pos, 2), lax.div(pos, 2)
    chips = n_seq // 2
    partner = chip * 2 + 1 - core
    barrier = pltpu.get_barrier_semaphore()

    def greet(axis, mine):
        def body(j, carry):
            @pl.when(j != mine)
            def _():
                pl.semaphore_signal(barrier, inc=1, device_id={axis: j}, device_id_type=MESH)

            return carry

        return body

    lax.fori_loop(0, n_seq, greet("seq", pos), 0)
    lax.fori_loop(0, n_dp, greet("dp", dpi), 0)

    def cols(h):
        return pl.ds(pl.multiple_of(h * size, size), size)

    def episode(place):
        total = 0
        for b in range(bounds_ref.shape[0]):
            total = total + (bounds_ref[b] <= place).astype(jnp.int32)
        return total

    first = pos * tok
    line = lax.broadcasted_iota(jnp.int32, (heads, tok), 0)
    level_int = jnp.zeros((heads, tok), jnp.int32)
    for h in range(heads):
        level_int = jnp.where(line == h, dec_ref[h], level_int)
    level = level_int.astype(F32)
    stream = float(tok * n_seq)
    lowest = math.log(4.0 / stream)
    slow = -0.25 * jnp.exp(level / 7.0 * math.log(8.0)) / stream
    fast = -jnp.exp(lowest + (level - 8.0) / 7.0 * (math.log(1.0 / 32.0) - lowest))
    rates = jnp.where(level_int < 8, slow, fast)
    for h in range(heads):
        rate_ref[h] = rates[h : h + 1]
    for c in range(2):
        start = (chip * 2 + c) * tok
        whole = (episode(start + tok - 1) == episode(start - 1)).astype(F32)
        passing = jnp.exp(rates[:, :size] * float(tok)) * whole
        for h in range(heads):
            pass_ref[c, h] = passing[h : h + 1]
    t_col = lax.broadcasted_iota(jnp.int32, (tok, size), 0)
    e_col = episode(first + t_col)
    t_val = t_col.astype(F32)
    enter_ref[...] = jnp.where(e_col == episode(first - 1), t_val + 1.0, FAR)
    leave_ref[...] = jnp.where(e_col == episode(first + tok - 1), tok - 1.0 - t_val, FAR)

    def decay(h, where_ref):
        return jnp.exp(rate_ref[h][:, :size] * where_ref[...])

    def local_state(h, a_ref, where_ref, b_ref):
        scaled = (decay(h, where_ref) * a_ref[:, cols(h)].astype(F32)).astype(BF16)
        return dot(scaled, b_ref[:, cols(h)], TN)

    theirs, own = (1 - core) * half, core * half

    def remote(src, dst, send, recv, target):
        return pltpu.make_async_remote_copy(
            src_ref=src, dst_ref=dst, send_sem=send, recv_sem=recv,
            device_id=target, device_id_type=MESH,
        )

    def l_copy(bufs, sem, i):
        return remote(bufs[0].at[i], bufs[2].at[i], sem.at[0, i], sem.at[1, i], {"seq": partner})

    def x_copy(bufs, sem, i, r, step):
        part = pl.ds(r * rows, rows)
        return remote(
            bufs[4].at[i, part], bufs[3].at[i, part],
            sem.at[0, i * CHUNKS + r], sem.at[1, i * CHUNKS + r], {"seq": pos + 2 * step},
        )

    def s_copy(bufs, sem, i, r):
        part = pl.ds(r * rows, rows)
        return remote(
            bufs[5].at[i, part], bufs[6].at[i, part],
            sem.at[0, i * CHUNKS + r], sem.at[1, i * CHUNKS + r], {"seq": partner},
        )

    def chain(bufs, l_sem, x_sem, s_sem, step, target_ref):
        if step > 0:
            rel, has_up, has_down = core, chip > 0, chip < chips - 1
            near, distant = 0, 1
        else:
            rel, has_up, has_down = 1 - core, chip < chips - 1, chip > 0
            near, distant = 1, 0
        lo, lr, x_in, xs, ss = bufs[1], bufs[2], bufs[3], bufs[4], bufs[5]
        is_near = rel == 0

        def body(i, carry):
            h = own + i
            l_copy(bufs, l_sem, i).wait_recv()
            pa = pass_ref[near, h]
            pb = pass_ref[distant, h]
            for r in range(CHUNKS):
                part = pl.ds(r * rows, rows)

                @pl.when(has_up)
                def _():
                    x_copy(bufs, x_sem, i, r, step).wait_recv()

                @pl.when(jnp.logical_not(has_up))
                def _():
                    x_in[i, part, :] = jnp.zeros((rows, size), F32)

                x, mine, other = x_in[i, part, :], lo[i, part, :], lr[i, part, :]
                la, lb = jnp.where(is_near, mine, other), jnp.where(is_near, other, mine)
                after = pa * x + la
                xs[i, part, :] = pb * after + lb

                @pl.when(has_down)
                def _():
                    x_copy(bufs, x_sem, i, r, step).start()

                ss[i, part, :] = jnp.where(is_near, after, x)
                s_copy(bufs, s_sem, i, r).start()
                target_ref[h, part, :] = jnp.where(is_near, x, after).astype(BF16)
            return carry

        lax.fori_loop(0, half, body, 0)

        return has_down

    def take_partner(bufs, s_sem, target_ref, i):
        for r in range(CHUNKS):
            s_copy(bufs, s_sem, i, r).wait_recv()
        target_ref[theirs + i] = bufs[6][i].astype(BF16)

    def finish(bufs, l_sem, x_sem, s_sem, step, has_down):
        def body(i, carry):
            l_copy(bufs, l_sem, i).wait_send()
            for r in range(CHUNKS):
                s_copy(bufs, s_sem, i, r).wait_send()

                @pl.when(has_down)
                def _():
                    x_copy(bufs, x_sem, i, r, step).wait_send()

            return carry

        lax.fori_loop(0, half, body, 0)

    fwd = (f_ls, f_lo, f_lr, f_x, f_xs, f_ss, f_sr)
    bwd = (b_ls, b_lo, b_lr, b_x, b_xs, b_ss, b_sr)

    def fwd_theirs(i, carry):
        f_ls[i] = local_state(theirs + i, k_ref, leave_ref, v_ref)
        return carry

    lax.fori_loop(0, half, fwd_theirs, 0)
    pl.semaphore_wait(barrier, n_seq - 1 + n_dp - 1)

    def fwd_own(i, carry):
        l_copy(fwd, f_l_sem, i).start()
        f_lo[i] = local_state(own + i, k_ref, leave_ref, v_ref)
        return carry

    lax.fori_loop(0, half, fwd_own, 0)

    t_full = lax.broadcasted_iota(jnp.int32, (tok, tok), 0)
    s_full = lax.broadcasted_iota(jnp.int32, (tok, tok), 1)
    e_row = episode(first + lax.broadcasted_iota(jnp.int32, (1, tok), 1))
    e_tall = episode(first + lax.broadcasted_iota(jnp.int32, (tok, 1), 0))
    allowed = (t_full >= s_full) & (e_row == e_tall)
    early, late = pl.ds(0, mid), pl.ds(mid, mid)

    def weights(h):
        rate = rate_ref[h]
        top = jnp.exp(rate[:, :mid] * dist_ref[0:mid, 0:mid])
        low = jnp.exp(rate * dist_ref[mid:tok, :])
        return top, low

    def intra(h, carry):
        c = cols(h)
        top, low = weights(h)
        k_all = k_ref[:, c]
        a_top = (dot(q_ref[early, c], k_ref[early, c], NT) * top).astype(BF16)
        a_low = (dot(q_ref[late, c], k_all, NT) * low).astype(BF16)
        mix_ref[h, 0:mid, 0:mid] = a_top
        mix_ref[h, mid:tok, :] = a_low
        o_ref[early, c] = dot(a_top, v_ref[early, c], NN)
        o_ref[late, c] = dot(a_low, v_ref[:, c], NN)
        return carry

    f_before = jnp.minimum(chip * HEADS_PER_HOP, heads)
    dist_ref[...] = jnp.where(allowed, (t_full - s_full).astype(F32), FAR)
    lax.fori_loop(0, f_before, intra, 0)
    f_down = chain(fwd, f_l_sem, f_x_sem, f_s_sem, 1, low_ref)
    lax.fori_loop(f_before, heads, intra, 0)

    sq_ref[...] = jnp.zeros_like(sq_ref)
    cr_ref[...] = jnp.zeros_like(cr_ref)

    def outputs(h):
        c = cols(h)
        o = o_ref[:, c] + decay(h, enter_ref) * dot(q_ref[:, c], low_ref[h], NN)
        o_ref[:, c] = o
        sq_ref[...] += o * o
        cr_ref[...] += g_ref[:, c].astype(F32) * gain_ref[pl.ds(h, 1), :] * o

    def out_own(i, carry):
        outputs(own + i)
        return carry

    def out_theirs(i, carry):
        take_partner(fwd, f_s_sem, low_ref, i)
        outputs(theirs + i)
        return carry

    lax.fori_loop(0, half, out_own, 0)
    lax.fori_loop(0, half, out_theirs, 0)

    sq_row = jnp.sum(jnp.transpose(sq_ref[...]), axis=0, keepdims=True)
    cr_row = jnp.sum(jnp.transpose(cr_ref[...]), axis=0, keepdims=True)
    line8 = lax.broadcasted_iota(jnp.int32, (8, tok), 0)
    stat_ref[dpi] = jnp.where(line8 == 0, sq_row, jnp.where(line8 == 1, cr_row, 0.0))

    def stat_copy(j, slot):
        return remote(
            stat_ref.at[slot], stat_ref.at[slot], stat_sem.at[0, j], stat_sem.at[1, slot],
            {"dp": j},
        )

    def stat_send(j, carry):
        @pl.when(j != dpi)
        def _():
            stat_copy(j, dpi).start()

        return carry

    def stat_recv(j, carry):
        @pl.when(j != dpi)
        def _():
            stat_copy(j, j).wait_recv()

        return carry

    def stat_done(j, carry):
        @pl.when(j != dpi)
        def _():
            stat_copy(j, dpi).wait_send()

        return carry

    lax.fori_loop(0, n_dp, stat_send, 0)
    lax.fori_loop(0, n_dp, stat_recv, 0)
    total = stat_ref[0]
    for j in range(1, n_dp):
        total = total + stat_ref[j]
    features = float(heads * size * n_dp)
    inv_row = lax.rsqrt(total[0:1, :] / features + 1e-06)
    mean_row = inv_row * total[1:2, :] / features
    sq_ref[...] = jnp.transpose(jnp.broadcast_to(inv_row, (size, tok)))
    cr_ref[...] = jnp.transpose(jnp.broadcast_to(mean_row, (size, tok)))

    def norm_grad(h):
        c = cols(h)
        inv = sq_ref[...]
        grad = g_ref[:, c].astype(F32)
        normed = inv * o_ref[:, c]
        do_ref[:, c] = (inv * (grad * gain_ref[pl.ds(h, 1), :] - normed * cr_ref[...])).astype(BF16)
        gsrc_ref[h] = jnp.sum((grad * normed).reshape(tok // 8, 8, size), axis=0)

    def bwd_theirs(i, carry):
        norm_grad(theirs + i)
        b_ls[i] = local_state(theirs + i, q_ref, enter_ref, do_ref)
        l_copy(bwd, b_l_sem, i).start()
        return carry

    def bwd_own(i, carry):
        norm_grad(own + i)
        b_lo[i] = local_state(own + i, q_ref, enter_ref, do_ref)
        return carry

    lax.fori_loop(0, half, bwd_theirs, 0)
    lax.fori_loop(0, half, bwd_own, 0)

    def gain_copy(j, slot):
        return remote(
            gsrc_ref.at[j], grecv_ref.at[slot], gain_sem.at[0, j], gain_sem.at[1, slot],
            {"seq": j},
        )

    def gain_send(j, carry):
        @pl.when(j != pos)
        def _():
            gain_copy(j, pos).start()

        return carry

    def gain_recv(j, carry):
        @pl.when(j != pos)
        def _():
            gain_copy(j, j).wait_recv()
            gain_copy(j, pos).wait_send()

        return carry

    def intra_grad(h, carry):
        c = cols(h)
        top, low = weights(h)
        q0, q1 = q_ref[early, c], q_ref[late, c]
        d0, d1 = do_ref[early, c], do_ref[late, c]
        da_top = (dot(d0, v_ref[early, c], NT) * top).astype(BF16)
        da_low = (dot(d1, v_ref[:, c], NT) * low).astype(BF16)
        enter = decay(h, enter_ref)
        state = low_ref[h]
        dq_ref[early, c] = (
            dot(da_top, k_ref[early, c], NN) + enter[:mid] * dot(d0, state, NT)
        ).astype(BF16)
        dq_ref[late, c] = (
            dot(da_low, k_ref[:, c], NN) + enter[mid:] * dot(d1, state, NT)
        ).astype(BF16)
        dki_ref[early, c] = dot(da_top, q0, TN) + dot(da_low[:, :mid], q1, TN)
        dki_ref[late, c] = dot(da_low[:, mid:], q1, TN)
        dvi_ref[early, c] = dot(mix_ref[h, 0:mid, 0:mid], d0, TN) + dot(
            mix_ref[h, mid:tok, 0:mid], d1, TN
        )
        dvi_ref[late, c] = dot(mix_ref[h, mid:tok, mid:tok], d1, TN)
        return carry

    b_before = jnp.minimum((chips - 1 - chip) * HEADS_PER_HOP, heads)
    lax.fori_loop(0, b_before, intra_grad, 0)
    b_down = chain(bwd, b_l_sem, b_x_sem, b_s_sem, -1, dlow_ref)
    if scatter:
        lax.fori_loop(0, n_seq, gain_send, 0)
    lax.fori_loop(b_before, heads, intra_grad, 0)

    def final(h):
        c = cols(h)
        leave = decay(h, leave_ref)
        state = dlow_ref[h]
        dk_ref[:, c] = (dki_ref[:, c] + leave * dot(v_ref[:, c], state, NT)).astype(BF16)
        dv_ref[:, c] = (dvi_ref[:, c] + leave * dot(k_ref[:, c], state, NN)).astype(BF16)

    def final_own(i, carry):
        final(own + i)
        return carry

    def final_theirs(i, carry):
        take_partner(bwd, b_s_sem, dlow_ref, i)
        final(theirs + i)
        return carry

    lax.fori_loop(0, half, final_own, 0)
    lax.fori_loop(0, half, final_theirs, 0)

    if scatter:
        grecv_ref[pos] = gsrc_ref[pos]
        lax.fori_loop(0, n_seq, gain_recv, 0)
        gain_sum = grecv_ref[0]
        for j in range(1, n_seq):
            gain_sum = gain_sum + grecv_ref[j]
        gg_ref[...] = jnp.sum(gain_sum, axis=0, keepdims=True)
    else:
        for h in range(heads):
            gg_ref[h : h + 1, :] = jnp.sum(gsrc_ref[h], axis=0, keepdims=True)
    finish(fwd, f_l_sem, f_x_sem, f_s_sem, 1, f_down)
    finish(bwd, b_l_sem, b_x_sem, b_s_sem, -1, b_down)
    lax.fori_loop(0, n_dp, stat_done, 0)


def shards(queries, keys, values, out_grad, gain, decay_index, bounds):
    tok, width = queries.shape
    heads = decay_index.shape[0]
    size = width // heads
    n_seq, n_dp = lax.axis_size("seq"), lax.axis_size("dp")
    half = heads // 2
    scatter = n_seq == heads
    cfg = (tok, heads, size, n_seq, n_dp, scatter)
    vmem = pl.BlockSpec(memory_space=pltpu.VMEM)
    smem = pl.BlockSpec(memory_space=pltpu.SMEM)
    state = pltpu.VMEM((half, size, size), F32)
    dma = pltpu.SemaphoreType.DMA
    chain_sems = [dma((2, half)), dma((2, half * CHUNKS)), dma((2, half * CHUNKS))]
    grads = jax.ShapeDtypeStruct((tok, width), BF16)
    query_grad, key_grad, value_grad, gain_part = pl.pallas_call(
        functools.partial(kernel, cfg),
        out_shape=[
            grads,
            grads,
            grads,
            jax.ShapeDtypeStruct((1 if scatter else heads, size), F32),
        ],
        in_specs=[vmem] * 5 + [smem] * 2,
        out_specs=[vmem] * 4,
        scratch_shapes=[
            pltpu.VMEM((heads, 1, tok), F32),
            pltpu.VMEM((2, heads, 1, size), F32),
            pltpu.VMEM((tok, size), F32),
            pltpu.VMEM((tok, size), F32),
            pltpu.VMEM((tok, tok), F32),
            pltpu.VMEM((heads, tok, tok), BF16),
            pltpu.VMEM((tok, width), F32),
            pltpu.VMEM((tok, width), BF16),
            pltpu.VMEM((tok, width), F32),
            pltpu.VMEM((tok, width), F32),
            pltpu.VMEM((heads, size, size), BF16),
            pltpu.VMEM((heads, size, size), BF16),
            pltpu.VMEM((tok, size), F32),
            pltpu.VMEM((tok, size), F32),
            pltpu.VMEM((n_dp, 8, tok), F32),
            pltpu.VMEM((heads, 8, size), F32),
            pltpu.VMEM((n_seq, 8, size), F32),
        ]
        + [state] * 14
        + chain_sems * 2
        + [dma((2, n_dp)), dma((2, n_seq))],
        compiler_params=pltpu.CompilerParams(
            collective_id=0, has_side_effects=True, vmem_limit_bytes=60 * 1024 * 1024
        ),
    )(queries, keys, values, out_grad, gain.reshape(heads, size), decay_index, bounds)
    if scatter:
        gain_grad = gain_part.reshape(-1)
    else:
        gain_grad = lax.psum_scatter(
            gain_part.reshape(-1), "seq", scatter_dimension=0, tiled=True
        )
    return query_grad, key_grad, value_grad, gain_grad


def solution(mesh):
    return jax.shard_map(
        shards,
        mesh=mesh,
        in_specs=(
            P("seq", "dp"),
            P("seq", "dp"),
            P("seq", "dp"),
            P("seq", "dp"),
            P("dp"),
            P("dp"),
            P(),
        ),
        out_specs=(P("seq", "dp"), P("seq", "dp"), P("seq", "dp"), P(("dp", "seq"))),
        check_vma=False,
    )
```

time: 183 us -> 57.3 us (0.31)
  blocking collectives: 51.3 us -> 0 us
  Pallas kernels: 0 us -> 51 us
  waiting for transfers between devices: 35.4 us -> 0 us
  matrix products: 31 us -> 0 us
  other arithmetic: 28.2 us -> 0 us
  between operations: 17 us -> 0.65 us
  local copies, waits for them, and re-layouts: 17.8 us -> 5.44 us
    pallas_call x0 -> x1, Pallas kernels: none -> 51 us  [shards(): pl.pallas_call(functools.partial(kernel, cfg), out_shape=[grads, grads, g...]
    all_gather x2 -> x0, waiting for transfers between devices: 35.4 us -> none  [carried_in(): everything = jax.tree.map(lambda part: lax.all_gather(part, axis), array)]
    unnamed x2 -> x0, blocking collectives: 33.5 us -> none
    dot_general x12 -> x0, matrix products: 31 us -> none  [the longest x1 4.28 us: shards(): jnp.einsum('hts,thf->shf', mixing, grad_mixed, preferred_element_type=jnp...]
    select_n x16 -> x0, other arithmetic: 18.8 us -> none  [hop(): return jax.tree.map(lambda a, b: jnp.where(reached, a, b), new, before)]
    psum x2 -> x0, blocking collectives: 17.8 us -> none  [the longest x1 9.81 us: shards(): square_total = lax.psum(jnp.sum(flat * flat, axis=1), 'dp')]
    unnamed x36 -> x10, local copies, waits for them, and re-layouts: 12.5 us -> 5.44 us
    reshape x2 -> x0, local copies, waits for them, and re-layouts: 4.49 us -> none  [the longest x1 3 us: shards(): flat = attended.reshape(tok_rows, feature_width)]
  transfers between devices with their start and end apart: 2 -> 0, of which waited for: 2 -> 0; matrix products, arithmetic and copies ran while one was open for 13% -> 0% of each run, Pallas kernels for 0% -> 0%
where the time goes in v1:
time: 57.3 us; the launch traced here: 57.1 us
  Pallas kernels  51 us (89%)
  local copies, waits for them, and re-layouts  5.44 us (9%)
  between operations  0.65 us (1%)
    pallas_call x1, Pallas kernels, shards(): pl.pallas_call(functools.partial(kernel, cfg), out_shape=[grads, grads, g...  51 us
    unnamed x10, local copies, waits for them, and re-layouts  5.44 us

profile of v1, /device:TPU:0, one launch (start us, length us, event | category | flops | bytes accessed | tf_op | source)
XLA Modules:
  0.0 57.1 jit_solution(7621528552562065022)
XLA Ops:
  0.6 51.0 %shard_map.102 = (bf16[512,1024]{1,0:T(8,128)(2,1)}, bf16[512,1024]{1,0:T(8,128)(2,1)}, bf16[512,1024]{1,0:T(8,128)(2,1)}, f32[1,128]{1,0:T(1,128)}) custom-call(bf16[512,1024]{1,0:T(8,128)(2,1)} %q_ref.1, bf16[512,1024]{1,0:T(8,128)(2,1)} %k_ref.1, bf16[512,1024]{1,0:T(8,128)(2,1)} %v_ref.1, bf16[512,1024]{1,0:T(8,128)(2,1)} %g_ref.1, f32[8,128]{1,0:T(8,128)} %bitcast.2, ...), custom_call_target="tpu_custom_call" | custom-call | tf_op jit(solution)/shard_map/pallas_call | solution.py:422
  51.6 0.0 copy-start.1
  51.7 2.4 %copy.15 = bf16[512,1024]{1,0:T(8,128)(2,1)} copy(bf16[512,1024]{1,0:T(8,128)(2,1)} %get-tuple-element.16) | data formatting | bytes 2097152
  54.0 0.0 copy-done.1
  54.0 0.0 copy-start
  54.0 1.0 %copy.16 = bf16[512,1024]{1,0:T(8,128)(2,1)} copy(bf16[512,1024]{1,0:T(8,128)(2,1)S(1)} %copy-done.1) | data formatting | bytes 2097152
  55.0 0.6 %copy-done = bf16[512,1024]{1,0:T(8,128)(2,1)S(1)} copy-done((bf16[512,1024]{1,0:T(8,128)(2,1)S(1)}, bf16[512,1024]{1,0:T(8,128)(2,1)}, u32[]{:S(2)}) %copy-start) | copy-done | bytes 1048600
  55.6 0.0 copy-start.2
  55.6 1.0 %copy.17 = bf16[512,1024]{1,0:T(8,128)(2,1)} copy(bf16[512,1024]{1,0:T(8,128)(2,1)S(1)} %copy-done) | data formatting | bytes 2097152
  56.6 0.0 copy-done.2
  56.6 0.5 copy.18
Async XLA Ops:
  51.6 2.4 %copy-start.1 = (bf16[512,1024]{1,0:T(8,128)(2,1)S(1)}, bf16[512,1024]{1,0:T(8,128)(2,1)}, u32[]{:S(2)}) copy-start(bf16[512,1024]{1,0:T(8,128)(2,1)} %get-tuple-element.17) | copy-start | bytes 3145732
  54.0 1.6 %copy-start = (bf16[512,1024]{1,0:T(8,128)(2,1)S(1)}, bf16[512,1024]{1,0:T(8,128)(2,1)}, u32[]{:S(2)}) copy-start(bf16[512,1024]{1,0:T(8,128)(2,1)} %get-tuple-element.18) | copy-start | bytes 3145732
  55.6 1.0 %copy-start.2 = (f32[1,128]{1,0:T(1,128)S(1)}, f32[1,128]{1,0:T(1,128)}, u32[]{:S(2)}) copy-start(f32[1,128]{1,0:T(1,128)} %get-tuple-element.11) | copy-start | bytes 1540

commit v2 on v1

--- a/solution.py
+++ b/solution.py
@@ -11,8 +11,10 @@
 MESH = pl.DeviceIdType.MESH
 F32, BF16 = jnp.float32, jnp.bfloat16
 FAR = 1e30
-CHUNKS = 2
-HEADS_PER_HOP = 2
+CHUNKS = 4
+FWD_PER_HOP = 4
+BWD_PER_HOP = 3
+FINAL_HEADS = 4
 
 NN = (((1,), (0,)), ((), ()))
 NT = (((1,), (1,)), ((), ()))
@@ -23,16 +25,53 @@
     return lax.dot_general(a, b, dims, preferred_element_type=F32)
 
 
+def decay_rates(level_int, stream):
+    level = level_int.astype(F32)
+    lowest = math.log(4.0 / stream)
+    slow = -0.25 * jnp.exp(level / 7.0 * math.log(8.0)) / stream
+    fast = -jnp.exp(lowest + (level - 8.0) / 7.0 * (math.log(1.0 / 32.0) - lowest))
+    return jnp.where(level_int < 8, slow, fast)
+
+
+def episode_of(bounds_ref, place):
+    total = 0
+    for b in range(bounds_ref.shape[0]):
+        total = total + (bounds_ref[b] <= place).astype(jnp.int32)
+    return total
+
+
+def final_kernel(
+    cfg, dec_ref, bounds_ref, k_ref, v_ref, dqi_ref, dki_ref, dvi_ref, dlow_ref, ggi_ref,
+    dq_ref, dk_ref, dv_ref, gg_ref,
+):
+    tok, size, n_seq = cfg
+    first = lax.axis_index("seq") * tok
+    t_col = lax.broadcasted_iota(jnp.int32, (tok, size), 0)
+    same = episode_of(bounds_ref, first + t_col) == episode_of(bounds_ref, first + tok - 1)
+    leave_pos = jnp.where(same, tok - 1.0 - t_col.astype(F32), FAR)
+    dq_ref[...] = dqi_ref[...]
+    gg_ref[...] = ggi_ref[...]
+    for u in range(FINAL_HEADS):
+        level = jnp.full((1, size), dec_ref[pl.program_id(0) * FINAL_HEADS + u], jnp.int32)
+        leave = jnp.exp(decay_rates(level, float(tok * n_seq)) * leave_pos)
+        c = slice(u * size, (u + 1) * size)
+        state = dlow_ref[u]
+        dk_ref[:, c] = (dki_ref[:, c].astype(F32) + leave * dot(v_ref[:, c], state, NT)).astype(BF16)
+        dv_ref[:, c] = (dvi_ref[:, c].astype(F32) + leave * dot(k_ref[:, c], state, NN)).astype(BF16)
+
+
 def kernel(
     cfg,
-    q_ref, k_ref, v_ref, g_ref, gain_ref, dec_ref, bounds_ref,
-    dq_ref, dk_ref, dv_ref, gg_ref,
+    q_hbm, k_hbm, v_hbm, g_hbm, gain_ref, dec_ref, bounds_ref,
+    dq_hbm, dki_hbm, dvi_hbm, dlow_hbm, gg_ref,
+    q_ref, k_ref, v_ref, g_ref, dq_ref,
     rate_ref, pass_ref, enter_ref, leave_ref, dist_ref,
     mix_ref, o_ref, do_ref, dki_ref, dvi_ref, low_ref, dlow_ref,
     sq_ref, cr_ref, stat_ref, gsrc_ref, grecv_ref,
     f_ls, f_lo, f_lr, f_x, f_xs, f_ss, f_sr,
     b_ls, b_lo, b_lr, b_x, b_xs, b_ss, b_sr,
     f_l_sem, f_x_sem, f_s_sem, b_l_sem, b_x_sem, b_s_sem, stat_sem, gain_sem,
+    in_sem, out_sem,
 ):
     tok, heads, size, n_seq, n_dp, scatter = cfg
     half, mid = heads // 2, tok // 2
@@ -41,6 +80,14 @@
     core, chip = lax.rem(pos, 2), lax.div(pos, 2)
     chips = n_seq // 2
     partner = chip * 2 + 1 - core
+    loads = [
+        pltpu.make_async_copy(src, dst, in_sem.at[i])
+        for i, (src, dst) in enumerate(
+            ((k_hbm, k_ref), (v_hbm, v_ref), (q_hbm, q_ref), (g_hbm, g_ref))
+        )
+    ]
+    for load in loads:
+        load.start()
     barrier = pltpu.get_barrier_semaphore()
 
     def greet(axis, mine):
@@ -60,22 +107,14 @@
         return pl.ds(pl.multiple_of(h * size, size), size)
 
     def episode(place):
-        total = 0
-        for b in range(bounds_ref.shape[0]):
-            total = total + (bounds_ref[b] <= place).astype(jnp.int32)
-        return total
+        return episode_of(bounds_ref, place)
 
     first = pos * tok
     line = lax.broadcasted_iota(jnp.int32, (heads, tok), 0)
     level_int = jnp.zeros((heads, tok), jnp.int32)
     for h in range(heads):
         level_int = jnp.where(line == h, dec_ref[h], level_int)
-    level = level_int.astype(F32)
-    stream = float(tok * n_seq)
-    lowest = math.log(4.0 / stream)
-    slow = -0.25 * jnp.exp(level / 7.0 * math.log(8.0)) / stream
-    fast = -jnp.exp(lowest + (level - 8.0) / 7.0 * (math.log(1.0 / 32.0) - lowest))
-    rates = jnp.where(level_int < 8, slow, fast)
+    rates = decay_rates(level_int, float(tok * n_seq))
     for h in range(heads):
         rate_ref[h] = rates[h : h + 1]
     for c in range(2):
@@ -122,56 +161,53 @@
             sem.at[0, i * CHUNKS + r], sem.at[1, i * CHUNKS + r], {"seq": partner},
         )
 
-    def chain(bufs, l_sem, x_sem, s_sem, step, target_ref):
+    def direction(step):
         if step > 0:
-            rel, has_up, has_down = core, chip > 0, chip < chips - 1
-            near, distant = 0, 1
-        else:
-            rel, has_up, has_down = 1 - core, chip < chips - 1, chip > 0
-            near, distant = 1, 0
+            return core, chip > 0, chip < chips - 1
+        return 1 - core, chip < chips - 1, chip > 0
+
+    def chain_step(bufs, sems, step, target_ref, i):
+        rel, has_up, has_down = direction(step)
+        near, distant = (0, 1) if step > 0 else (1, 0)
+        l_sem, x_sem, s_sem = sems
         lo, lr, x_in, xs, ss = bufs[1], bufs[2], bufs[3], bufs[4], bufs[5]
         is_near = rel == 0
-
-        def body(i, carry):
-            h = own + i
-            l_copy(bufs, l_sem, i).wait_recv()
-            pa = pass_ref[near, h]
-            pb = pass_ref[distant, h]
-            for r in range(CHUNKS):
-                part = pl.ds(r * rows, rows)
-
-                @pl.when(has_up)
-                def _():
-                    x_copy(bufs, x_sem, i, r, step).wait_recv()
-
-                @pl.when(jnp.logical_not(has_up))
-                def _():
-                    x_in[i, part, :] = jnp.zeros((rows, size), F32)
-
-                x, mine, other = x_in[i, part, :], lo[i, part, :], lr[i, part, :]
-                la, lb = jnp.where(is_near, mine, other), jnp.where(is_near, other, mine)
-                after = pa * x + la
-                xs[i, part, :] = pb * after + lb
-
-                @pl.when(has_down)
-                def _():
-                    x_copy(bufs, x_sem, i, r, step).start()
-
-                ss[i, part, :] = jnp.where(is_near, after, x)
-                s_copy(bufs, s_sem, i, r).start()
-                target_ref[h, part, :] = jnp.where(is_near, x, after).astype(BF16)
-            return carry
-
-        lax.fori_loop(0, half, body, 0)
-
-        return has_down
+        h = own + i
+        l_copy(bufs, l_sem, i).wait_recv()
+        pa, pb = pass_ref[near, h], pass_ref[distant, h]
+        for r in range(CHUNKS):
+            part = pl.ds(r * rows, rows)
+
+            @pl.when(has_up)
+            def _():
+                x_copy(bufs, x_sem, i, r, step).wait_recv()
+
+            @pl.when(jnp.logical_not(has_up))
+            def _():
+                x_in[i, part, :] = jnp.zeros((rows, size), F32)
+
+            x, mine, other = x_in[i, part, :], lo[i, part, :], lr[i, part, :]
+            la, lb = jnp.where(is_near, mine, other), jnp.where(is_near, other, mine)
+            after = pa * x + la
+            xs[i, part, :] = pb * after + lb
+
+            @pl.when(has_down)
+            def _():
+                x_copy(bufs, x_sem, i, r, step).start()
+
+            ss[i, part, :] = jnp.where(is_near, after, x)
+            s_copy(bufs, s_sem, i, r).start()
+            target_ref[h, part, :] = jnp.where(is_near, x, after).astype(BF16)
 
     def take_partner(bufs, s_sem, target_ref, i):
         for r in range(CHUNKS):
             s_copy(bufs, s_sem, i, r).wait_recv()
         target_ref[theirs + i] = bufs[6][i].astype(BF16)
 
-    def finish(bufs, l_sem, x_sem, s_sem, step, has_down):
+    def finish(bufs, sems, step):
+        l_sem, x_sem, s_sem = sems
+        has_down = direction(step)[2]
+
         def body(i, carry):
             l_copy(bufs, l_sem, i).wait_send()
             for r in range(CHUNKS):
@@ -188,19 +224,29 @@
     fwd = (f_ls, f_lo, f_lr, f_x, f_xs, f_ss, f_sr)
     bwd = (b_ls, b_lo, b_lr, b_x, b_xs, b_ss, b_sr)
 
-    def fwd_theirs(i, carry):
+    fwd_sems = (f_l_sem, f_x_sem, f_s_sem)
+    bwd_sems = (b_l_sem, b_x_sem, b_s_sem)
+
+    f_head, b_head = chip == 0, chip == chips - 1
+    loads[0].wait()
+    loads[1].wait()
+    pl.semaphore_wait(barrier, n_seq - 1 + n_dp - 1)
+    for i in range(half):
         f_ls[i] = local_state(theirs + i, k_ref, leave_ref, v_ref)
-        return carry
-
-    lax.fori_loop(0, half, fwd_theirs, 0)
-    pl.semaphore_wait(barrier, n_seq - 1 + n_dp - 1)
-
-    def fwd_own(i, carry):
         l_copy(fwd, f_l_sem, i).start()
         f_lo[i] = local_state(own + i, k_ref, leave_ref, v_ref)
-        return carry
-
-    lax.fori_loop(0, half, fwd_own, 0)
+        if i > 0:
+
+            @pl.when(f_head)
+            def _():
+                chain_step(fwd, fwd_sems, 1, low_ref, i - 1)
+
+    @pl.when(f_head)
+    def _():
+        chain_step(fwd, fwd_sems, 1, low_ref, half - 1)
+
+    loads[2].wait()
+    loads[3].wait()
 
     t_full = lax.broadcasted_iota(jnp.int32, (tok, tok), 0)
     s_full = lax.broadcasted_iota(jnp.int32, (tok, tok), 1)
@@ -227,11 +273,10 @@
         o_ref[late, c] = dot(a_low, v_ref[:, c], NN)
         return carry
 
-    f_before = jnp.minimum(chip * HEADS_PER_HOP, heads)
+    f_before = jnp.minimum(chip * FWD_PER_HOP, heads)
+    f_full = f_before >= heads
     dist_ref[...] = jnp.where(allowed, (t_full - s_full).astype(F32), FAR)
     lax.fori_loop(0, f_before, intra, 0)
-    f_down = chain(fwd, f_l_sem, f_x_sem, f_s_sem, 1, low_ref)
-    lax.fori_loop(f_before, heads, intra, 0)
 
     sq_ref[...] = jnp.zeros_like(sq_ref)
     cr_ref[...] = jnp.zeros_like(cr_ref)
@@ -252,8 +297,23 @@
         outputs(theirs + i)
         return carry
 
-    lax.fori_loop(0, half, out_own, 0)
-    lax.fori_loop(0, half, out_theirs, 0)
+    def fwd_chain(i, carry):
+        chain_step(fwd, fwd_sems, 1, low_ref, i)
+
+        @pl.when(f_full)
+        def _():
+            out_own(i, 0)
+
+        @pl.when(f_full & (i > 0))
+        def _():
+            out_theirs(i - 1, 0)
+
+        return carry
+
+    lax.fori_loop(jnp.where(f_head, half, 0), half, fwd_chain, 0)
+    lax.fori_loop(f_before, heads, intra, 0)
+    lax.fori_loop(jnp.where(f_full, half, 0), half, out_own, 0)
+    lax.fori_loop(jnp.where(f_full, half - 1, 0), half, out_theirs, 0)
 
     sq_row = jnp.sum(jnp.transpose(sq_ref[...]), axis=0, keepdims=True)
     cr_row = jnp.sum(jnp.transpose(cr_ref[...]), axis=0, keepdims=True)
@@ -306,19 +366,21 @@
         do_ref[:, c] = (inv * (grad * gain_ref[pl.ds(h, 1), :] - normed * cr_ref[...])).astype(BF16)
         gsrc_ref[h] = jnp.sum((grad * normed).reshape(tok // 8, 8, size), axis=0)
 
-    def bwd_theirs(i, carry):
+    for i in range(half):
         norm_grad(theirs + i)
         b_ls[i] = local_state(theirs + i, q_ref, enter_ref, do_ref)
         l_copy(bwd, b_l_sem, i).start()
-        return carry
-
-    def bwd_own(i, carry):
         norm_grad(own + i)
         b_lo[i] = local_state(own + i, q_ref, enter_ref, do_ref)
-        return carry
-
-    lax.fori_loop(0, half, bwd_theirs, 0)
-    lax.fori_loop(0, half, bwd_own, 0)
+        if i > 0:
+
+            @pl.when(b_head)
+            def _():
+                chain_step(bwd, bwd_sems, -1, dlow_ref, i - 1)
+
+    @pl.when(b_head)
+    def _():
+        chain_step(bwd, bwd_sems, -1, dlow_ref, half - 1)
 
     def gain_copy(j, slot):
         return remote(
@@ -340,6 +402,18 @@
             gain_copy(j, pos).wait_send()
 
         return carry
+
+    def put(h):
+        c = cols(h)
+        return [
+            pltpu.make_async_copy(src.at[:, c], dst.at[:, c], out_sem.at[n, h])
+            for n, (src, dst) in enumerate(
+                ((dq_ref, dq_hbm), (dki_ref, dki_hbm), (dvi_ref, dvi_hbm))
+            )
+        ]
+
+    def put_state(h):
+        return pltpu.make_async_copy(dlow_ref.at[h], dlow_hbm.at[h], out_sem.at[3, h])
 
     def intra_grad(h, carry):
         c = cols(h)
@@ -356,39 +430,37 @@
         dq_ref[late, c] = (
             dot(da_low, k_ref[:, c], NN) + enter[mid:] * dot(d1, state, NT)
         ).astype(BF16)
-        dki_ref[early, c] = dot(da_top, q0, TN) + dot(da_low[:, :mid], q1, TN)
-        dki_ref[late, c] = dot(da_low[:, mid:], q1, TN)
-        dvi_ref[early, c] = dot(mix_ref[h, 0:mid, 0:mid], d0, TN) + dot(
-            mix_ref[h, mid:tok, 0:mid], d1, TN
-        )
-        dvi_ref[late, c] = dot(mix_ref[h, mid:tok, mid:tok], d1, TN)
-        return carry
-
-    b_before = jnp.minimum((chips - 1 - chip) * HEADS_PER_HOP, heads)
-    lax.fori_loop(0, b_before, intra_grad, 0)
-    b_down = chain(bwd, b_l_sem, b_x_sem, b_s_sem, -1, dlow_ref)
+        dki_ref[early, c] = (dot(da_top, q0, TN) + dot(da_low[:, :mid], q1, TN)).astype(BF16)
+        dki_ref[late, c] = dot(da_low[:, mid:], q1, TN).astype(BF16)
+        dvi_ref[early, c] = (
+            dot(mix_ref[h, 0:mid, 0:mid], d0, TN) + dot(mix_ref[h, mid:tok, 0:mid], d1, TN)
+        ).astype(BF16)
+        dvi_ref[late, c] = dot(mix_ref[h, mid:tok, mid:tok], d1, TN).astype(BF16)
+        for copy in put(h):
+            copy.start()
+        return carry
+
     if scatter:
         lax.fori_loop(0, n_seq, gain_send, 0)
+    b_before = jnp.minimum((chips - 1 - chip) * BWD_PER_HOP, heads)
+    lax.fori_loop(0, b_before, intra_grad, 0)
+
+    def bwd_theirs(i, carry):
+        take_partner(bwd, b_s_sem, dlow_ref, i)
+        put_state(theirs + i).start()
+        return carry
+
+    def bwd_chain(i, carry):
+        @pl.when(jnp.logical_not(b_head))
+        def _():
+            chain_step(bwd, bwd_sems, -1, dlow_ref, i)
+
+        put_state(own + i).start()
+        return carry
+
+    lax.fori_loop(0, half, bwd_chain, 0)
     lax.fori_loop(b_before, heads, intra_grad, 0)
-
-    def final(h):
-        c = cols(h)
-        leave = decay(h, leave_ref)
-        state = dlow_ref[h]
-        dk_ref[:, c] = (dki_ref[:, c] + leave * dot(v_ref[:, c], state, NT)).astype(BF16)
-        dv_ref[:, c] = (dvi_ref[:, c] + leave * dot(k_ref[:, c], state, NN)).astype(BF16)
-
-    def final_own(i, carry):
-        final(own + i)
-        return carry
-
-    def final_theirs(i, carry):
-        take_partner(bwd, b_s_sem, dlow_ref, i)
-        final(theirs + i)
-        return carry
-
-    lax.fori_loop(0, half, final_own, 0)
-    lax.fori_loop(0, half, final_theirs, 0)
+    lax.fori_loop(0, half, bwd_theirs, 0)
 
     if scatter:
         grecv_ref[pos] = gsrc_ref[pos]
@@ -400,8 +472,16 @@
     else:
         for h in range(heads):
             gg_ref[h : h + 1, :] = jnp.sum(gsrc_ref[h], axis=0, keepdims=True)
-    finish(fwd, f_l_sem, f_x_sem, f_s_sem, 1, f_down)
-    finish(bwd, b_l_sem, b_x_sem, b_s_sem, -1, b_down)
+    finish(fwd, fwd_sems, 1)
+    finish(bwd, bwd_sems, -1)
+
+    def put_done(h, carry):
+        for copy in put(h):
+            copy.wait()
+        put_state(h).wait()
+        return carry
+
+    lax.fori_loop(0, heads, put_done, 0)
     lax.fori_loop(0, n_dp, stat_done, 0)
 
 
@@ -414,22 +494,25 @@
     scatter = n_seq == heads
     cfg = (tok, heads, size, n_seq, n_dp, scatter)
     vmem = pl.BlockSpec(memory_space=pltpu.VMEM)
+    anywhere = pl.BlockSpec(memory_space=pl.ANY)
     smem = pl.BlockSpec(memory_space=pltpu.SMEM)
     state = pltpu.VMEM((half, size, size), F32)
     dma = pltpu.SemaphoreType.DMA
     chain_sems = [dma((2, half)), dma((2, half * CHUNKS)), dma((2, half * CHUNKS))]
     grads = jax.ShapeDtypeStruct((tok, width), BF16)
-    query_grad, key_grad, value_grad, gain_part = pl.pallas_call(
+    query_part, key_part, value_part, state_grad, gain_part = pl.pallas_call(
         functools.partial(kernel, cfg),
         out_shape=[
             grads,
             grads,
             grads,
+            jax.ShapeDtypeStruct((heads, size, size), BF16),
             jax.ShapeDtypeStruct((1 if scatter else heads, size), F32),
         ],
-        in_specs=[vmem] * 5 + [smem] * 2,
-        out_specs=[vmem] * 4,
-        scratch_shapes=[
+        in_specs=[anywhere] * 4 + [vmem] + [smem] * 2,
+        out_specs=[anywhere] * 4 + [vmem],
+        scratch_shapes=[pltpu.VMEM((tok, width), BF16)] * 5
+        + [
             pltpu.VMEM((heads, 1, tok), F32),
             pltpu.VMEM((2, heads, 1, size), F32),
             pltpu.VMEM((tok, size), F32),
@@ -438,8 +521,8 @@
             pltpu.VMEM((heads, tok, tok), BF16),
             pltpu.VMEM((tok, width), F32),
             pltpu.VMEM((tok, width), BF16),
-            pltpu.VMEM((tok, width), F32),
-            pltpu.VMEM((tok, width), F32),
+            pltpu.VMEM((tok, width), BF16),
+            pltpu.VMEM((tok, width), BF16),
             pltpu.VMEM((heads, size, size), BF16),
             pltpu.VMEM((heads, size, size), BF16),
             pltpu.VMEM((tok, size), F32),
@@ -450,11 +533,22 @@
         ]
         + [state] * 14
         + chain_sems * 2
-        + [dma((2, n_dp)), dma((2, n_seq))],
+        + [dma((2, n_dp)), dma((2, n_seq)), dma((4,)), dma((4, heads))],
         compiler_params=pltpu.CompilerParams(
             collective_id=0, has_side_effects=True, vmem_limit_bytes=60 * 1024 * 1024
         ),
     )(queries, keys, values, out_grad, gain.reshape(heads, size), decay_index, bounds)
+    wide = pl.BlockSpec((tok, FINAL_HEADS * size), lambda j: (0, j))
+    gain_spec = pl.BlockSpec(gain_part.shape, lambda j: (0, 0))
+    query_grad, key_grad, value_grad, gain_part = pl.pallas_call(
+        functools.partial(final_kernel, (tok, size, n_seq)),
+        grid=(heads // FINAL_HEADS,),
+        out_shape=[grads, grads, grads, jax.ShapeDtypeStruct(gain_part.shape, F32)],
+        in_specs=[smem] * 2
+        + [wide] * 5
+        + [pl.BlockSpec((FINAL_HEADS, size, size), lambda j: (j, 0, 0)), gain_spec],
+        out_specs=[wide] * 3 + [gain_spec],
+    )(decay_index, bounds, keys, values, query_part, key_part, value_part, state_grad, gain_part)
     if scatter:
         gain_grad = gain_part.reshape(-1)
     else:

time: 57.3 us -> 49.6 us (0.87)
  local copies, waits for them, and re-layouts: 5.44 us -> 0 us
  Pallas kernels: 51 us -> 48.3 us
    pallas_call x1, Pallas kernels: 51 us -> 44 us  [shards(): pl.pallas_call(functools.partial(kernel, cfg), out_shape=[grads, grads, g...]
    unnamed x10 -> x0, local copies, waits for them, and re-layouts: 5.44 us -> none
    pallas_call x0 -> x1, Pallas kernels: none -> 4.36 us  [shards(): pl.pallas_call(functools.partial(final_kernel, (tok, size, n_seq)), grid=...]
where the time goes in v2:
time: 49.6 us; the launch traced here: 49 us
  Pallas kernels  48.3 us (97%)
  between operations  0.64 us (1%)
    pallas_call x1, Pallas kernels, shards(): pl.pallas_call(functools.partial(kernel, cfg), out_shape=[grads, grads, g...  44 us
    pallas_call x1, Pallas kernels, shards(): pl.pallas_call(functools.partial(final_kernel, (tok, size, n_seq)), grid=...  4.36 us

profile of v2, /device:TPU:0, one launch (start us, length us, event | category | flops | bytes accessed | tf_op | source)
XLA Modules:
  0.0 49.0 jit_solution(18121867414659052288)
XLA Ops:
  0.6 44.0 %shard_map.102 = (bf16[512,1024]{1,0:T(8,128)(2,1)}, bf16[512,1024]{1,0:T(8,128)(2,1)}, bf16[512,1024]{1,0:T(8,128)(2,1)}, bf16[8,128,128]{2,1,0:T(8,128)(2,1)}, f32[1,128]{1,0:T(1,128)}) custom-call(bf16[512,1024]{1,0:T(8,128)(2,1)} %q_hbm.1, bf16[512,1024]{1,0:T(8,128)(2,1)} %k_ref.1, bf16[512,1024]{1,0:T(8,128)(2,1)} %v_ref.1, bf16[512,1024]{1,0:T(8,128)(2,1)} %g_hbm.1, ...), custom_call_target="tpu_custom_call" | custom-call | tf_op jit(solution)/shard_map/pallas_call | solution.py:503
  44.6 4.4 %shard_map.103 = (bf16[512,1024]{1,0:T(8,128)(2,1)}, bf16[512,1024]{1,0:T(8,128)(2,1)}, bf16[512,1024]{1,0:T(8,128)(2,1)}, f32[1,128]{1,0:T(1,128)}) custom-call(s32[8]{0:T(128)} %dec_ref.3, s32[3]{0:T(128)} %bounds_ref.3, bf16[512,1024]{1,0:T(8,128)(2,1)} %k_ref.1, bf16[512,1024]{1,0:T(8,128)(2,1)} %v_ref.1, bf16[512,1024]{1,0:T(8,128)(2,1)} %get-tuple-element.13.dqi_ref, ...), custom_call_target="tpu_custom_call" | custom-call | tf_op jit(solution)/shard_map/pallas_call | solution.py:543

commit v3 on v2

--- a/solution.py
+++ b/solution.py
@@ -230,9 +230,10 @@
     f_head, b_head = chip == 0, chip == chips - 1
     loads[0].wait()
     loads[1].wait()
-    pl.semaphore_wait(barrier, n_seq - 1 + n_dp - 1)
     for i in range(half):
         f_ls[i] = local_state(theirs + i, k_ref, leave_ref, v_ref)
+        if i == 0:
+            pl.semaphore_wait(barrier, n_seq - 1 + n_dp - 1)
         l_copy(fwd, f_l_sem, i).start()
         f_lo[i] = local_state(own + i, k_ref, leave_ref, v_ref)
         if i > 0:
@@ -456,11 +457,16 @@
             chain_step(bwd, bwd_sems, -1, dlow_ref, i)
 
         put_state(own + i).start()
+
+        @pl.when(i > 0)
+        def _():
+            bwd_theirs(i - 1, 0)
+
         return carry
 
     lax.fori_loop(0, half, bwd_chain, 0)
     lax.fori_loop(b_before, heads, intra_grad, 0)
-    lax.fori_loop(0, half, bwd_theirs, 0)
+    bwd_theirs(half - 1, 0)
 
     if scatter:
         grecv_ref[pos] = gsrc_ref[pos]

time: 49.6 us -> 49.5 us (level)
  no operation moved by 1% of the time
where the time goes in v3:
time: 49.5 us; the launch traced here: 48.9 us
  Pallas kernels  48.2 us (97%)
  between operations  0.64 us (1%)
    pallas_call x1, Pallas kernels, shards(): pl.pallas_call(functools.partial(kernel, cfg), out_shape=[grads, grads, g...  43.9 us
    pallas_call x1, Pallas kernels, shards(): pl.pallas_call(functools.partial(final_kernel, (tok, size, n_seq)), grid=...  4.37 us

profile of v3, /device:TPU:0, one launch (start us, length us, event | category | flops | bytes accessed | tf_op | source)
XLA Modules:
  0.0 48.9 jit_solution(263313926816369483)
XLA Ops:
  0.6 43.9 %shard_map.102 = (bf16[512,1024]{1,0:T(8,128)(2,1)}, bf16[512,1024]{1,0:T(8,128)(2,1)}, bf16[512,1024]{1,0:T(8,128)(2,1)}, bf16[8,128,128]{2,1,0:T(8,128)(2,1)}, f32[1,128]{1,0:T(1,128)}) custom-call(bf16[512,1024]{1,0:T(8,128)(2,1)} %q_hbm.1, bf16[512,1024]{1,0:T(8,128)(2,1)} %k_ref.1, bf16[512,1024]{1,0:T(8,128)(2,1)} %v_ref.1, bf16[512,1024]{1,0:T(8,128)(2,1)} %g_hbm.1, ...), custom_call_target="tpu_custom_call" | custom-call | tf_op jit(solution)/shard_map/pallas_call | solution.py:509
  44.5 4.4 %shard_map.103 = (bf16[512,1024]{1,0:T(8,128)(2,1)}, bf16[512,1024]{1,0:T(8,128)(2,1)}, bf16[512,1024]{1,0:T(8,128)(2,1)}, f32[1,128]{1,0:T(1,128)}) custom-call(s32[8]{0:T(128)} %dec_ref.3, s32[3]{0:T(128)} %bounds_ref.3, bf16[512,1024]{1,0:T(8,128)(2,1)} %k_ref.1, bf16[512,1024]{1,0:T(8,128)(2,1)} %v_ref.1, bf16[512,1024]{1,0:T(8,128)(2,1)} %get-tuple-element.13.dqi_ref, ...), custom_call_target="tpu_custom_call" | custom-call | tf_op jit(solution)/shard_map/pallas_call | solution.py:549
